TPU v7x, 1024 devices: a whole 4x4x32 slice. The times are simulated.
1024 devices in a mesh: pipe: 4 (over x), tensor: 32 (over z), dp: 8 (over y, core).
Axes of the slice: x: 4, y: 4, z: 32, core: 2. Of those that a mesh axis runs over, the one named last changes fastest.
Arguments:
- section_layers: int32 [4], replicated, may hold values from 9 to 11
- grad_out: bfloat16 [4, 8, 192, 4096], P('pipe', 'dp', 'tensor'), may hold values from -6 to 6
- gate_act: bfloat16 [4, 8, 192, 28672], P('pipe', 'dp', None, 'tensor'), may hold values from -6 to 6
- up_act: bfloat16 [4, 8, 192, 28672], P('pipe', 'dp', None, 'tensor'), may hold values from -6 to 6
- down_weight: bfloat16 [4, 28672, 4096], P('pipe', 'tensor'), may hold values from -0.09375 to 0.09375
Outputs:
- grad_gate: bfloat16 [4, 8, 192, 28672], P('pipe', 'dp', None, 'tensor')
- grad_up: bfloat16 [4, 8, 192, 28672], P('pipe', 'dp', None, 'tensor')
- grad_down_w: bfloat16 [4, 28672, 4096], P('pipe', ('tensor', 'dp'))
All inputs are finite; a program needn't handle non-finite values.
Results may differ from a plain program's by a relative error of at most 0.013.
Values may be sent and summed in bfloat16 or wider, within the bound.
A program may use at most 64 MiB of HBM per device.

v0:
```python
import jax
import jax.numpy as jnp
from jax import lax
from jax.sharding import PartitionSpec as P


def per_device(section_layers, grad_out, gate_act, up_act, down_weight):
    section = lax.axis_index("pipe")
    positions = jnp.arange(section_layers.shape[0], dtype=jnp.int32)
    offset = jnp.sum(jnp.where(positions < section, section_layers, 0))
    layers_here = jnp.sum(jnp.where(positions == section, section_layers, 0))
    scale = jnp.sqrt(10.0 / (offset + layers_here).astype(jnp.float32))
    gate = gate_act[0, 0].astype(jnp.float32)
    up = up_act[0, 0].astype(jnp.float32)
    logistic = jax.nn.sigmoid(gate)
    activated = gate * logistic
    hidden = (activated * up).astype(jnp.bfloat16)
    weight = down_weight[0]
    all_rows = lax.all_gather(grad_out[0, 0], "tensor", axis=0, tiled=True)
    grad_hidden = scale * lax.dot_general(
        all_rows, weight, (((1,), (1,)), ((), ())), preferred_element_type=jnp.float32
    )
    grad_gate = (grad_hidden * up * logistic * (1.0 + gate * (1.0 - logistic))).astype(jnp.bfloat16)
    grad_up = (grad_hidden * activated).astype(jnp.bfloat16)
    replicas = lax.axis_size("dp")
    norm_scale = scale / jnp.sqrt(jnp.float32(hidden.shape[0] * replicas))
    summed = lax.psum_scatter(
        (
            norm_scale
            * lax.dot_general(
                hidden, all_rows, (((0,), (0,)), ((), ())), preferred_element_type=jnp.float32
            )
        ).astype(jnp.bfloat16),
        "dp",
        scatter_dimension=0,
        tiled=True,
    )
    grad_down_w = summed[None]
    return (grad_gate[None, None], grad_up[None, None], grad_down_w)


def solution(mesh):
    placed = (
        P(),
        P("pipe", "dp", "tensor", None),
        P("pipe", "dp", None, "tensor"),
        P("pipe", "dp", None, "tensor"),
        P("pipe", "tensor", None),
    )
    return jax.shard_map(
        per_device,
        mesh=mesh,
        in_specs=placed,
        out_specs=(
            P("pipe", "dp", None, "tensor"),
            P("pipe", "dp", None, "tensor"),
            P("pipe", ("tensor", "dp"), None),
        ),
        check_vma=False,
    )
```

profile of v0, /device:TPU:6, one launch (start us, length us, event | category | flops | bytes accessed | tf_op | source)
XLA Modules:
  0.0 231.8 jit_solution(7514591038351808784)
XLA Ops:
  7.2 0.0 all-gather.3.cloned.1.call-start
  7.2 1.6 copy.9
  8.8 0.0 all-gather.3.cloned.1.call-update
  8.8 0.0 reduce-scatter.2.cloned.1.call-start
  8.8 1.3 fusion.24
  11.5 148.9 %all-gather.3.cloned.1.call-done = bf16[1,1,192,4096]{3,1,0,2:T(2,128)(2,1)} async-done(((bf16[1,1,6,4096]{3,1,0,2:T(2,128)(2,1)}), bf16[1,1,192,4096]{3,1,0,2:T(2,128)(2,1)}) %all-gather.3.cloned.1.call-update) | async-done | bytes 1572880 | tf_op jit(solution)/shard_map/all_gather | solution.py:19
  160.4 8.0 %multiply_convert_fusion = bf16[896,4096]{1,0:T(8,128)(2,1)} fusion(f32[]{:T(128)S(6)} %div.11, bf16[1,1,192,4096]{3,1,0,2:T(2,128)(2,1)} %all-gather.3.cloned.1.call-done, bf16[1,1,192,896]{3,2,1,0:T(8,128)(2,1)} %param.8, bf16[1,1,192,896]{3,2,1,0:T(8,128)(2,1)} %param.7), kind=kOutput, calls=%fused_computation | convolution fusion | flops 1418002432 | bytes 9601028 | tf_op jit(solution)/shard_map/dot_general | solution.py:30
  168.4 0.0 copy-start
  168.4 0.0 copy-start.1
  168.4 0.0 reduce-scatter.2.cloned.1.call-update
  168.4 1.9 copy-done
  170.3 0.0 copy-done.1
  170.3 7.6 %fusion.19 = (bf16[1,1,192,896]{3,2,1,0:T(8,128)(2,1)}, bf16[1,1,192,896]{3,2,1,0:T(8,128)(2,1)}) fusion(bf16[1,1,192,896]{3,2,1,0:T(8,128)(2,1)S(1)} %copy-done.1, bf16[1,1,192,896]{3,2,1,0:T(8,128)(2,1)} %param.8, bf16[1,896,4096]{2,1,0:T(8,128)(2,1)} %param.9, bf16[1,1,192,4096]{3,1,0,2:T(2,128)(2,1)S(1)} %copy-done, f32[]{:T(128)S(6)} %sqrt.3), kind=kOutput, calls=%fused_computation.22 | convolution fusion | flops 1412038656 | bytes 10289156 | tf_op jit(solution)/shard_map/dot_general | solution.py:20
  178.0 47.0 %reduce-scatter.2.cloned.1.call-done = bf16[112,4096]{1,0:T(8,128)(2,1)} async-done(((bf16[896,4096]{1,0:T(8,128)(2,1)}), bf16[112,4096]{1,0:T(8,128)(2,1)}) %reduce-scatter.2.cloned.1.call-update) | async-done | bytes 917520 | tf_op jit(solution)/shard_map/reduce_scatter | solution.py:27
Async XLA Ops:
  7.2 153.3 %all-gather.3.cloned.1.call-start = ((), (), s32[]{:S(2)}) async-start(), calls=%async_computation.2 | async-start | bytes 3244032 | tf_op jit(solution)/shard_map/all_gather | solution.py:19
  8.8 216.1 %reduce-scatter.2.cloned.1.call-start = ((), (), s32[]{:S(2)}) async-start(), calls=%async_computation.1 | async-start | bytes 8257536 | tf_op jit(solution)/shard_map/reduce_scatter | solution.py:27
  168.4 1.9 copy-start
  168.4 1.9 copy-start.1
Sparse Core Ops, SparseCore 0:
  11.2 149.1 all-gather.2
  168.6 56.3 reduce-scatter.1
where the time goes:
time: 232 us
  waiting for transfers between devices  196 us (84%)
  matrix products  15.6 us (7%)
  between operations  15.4 us (7%)
  local copies, waits for them, and re-layouts  3.45 us (1%)
    all_gather x1, waiting for transfers between devices, per_device(): all_rows = lax.all_gather(grad_out[0, 0], 'tensor', axis=0, tiled=True)  149 us
    reduce_scatter x1, waiting for transfers between devices, per_device(): lax.psum_scatter((norm_scale * lax.dot_general(hidden, all_rows, (((0,),...  47 us
    dot_general x1, matrix products, per_device(): lax.dot_general(hidden, all_rows, (((0,), (0,)), ((), ())), preferred_ele...  7.96 us
    dot_general x1, matrix products, per_device(): lax.dot_general(all_rows, weight, (((1,), (1,)), ((), ())), preferred_ele...  7.63 us
  transfers between devices with their start and end apart: 2, of which 2 were waited for; matrix products, arithmetic and copies ran while one was open for 4% of the time, Pallas kernels for 0%

commit v1 on v0

v1 whole, which is shorter than its diff:
```python
import functools

import jax
import jax.numpy as jnp
from jax import lax
from jax.experimental import pallas as pl
from jax.experimental.pallas import tpu as pltpu
from jax.sharding import PartitionSpec as P

MESH = pl.DeviceIdType.MESH
F32 = jnp.float32
BF16 = jnp.bfloat16
SPLITS = 2


def mm(a, b):
    return jnp.dot(a, b, preferred_element_type=F32)


def kernel(
    nz, npipe,
    layers_ref, go_hbm, gate_hbm, up_hbm, w_hbm,
    gg_ref, gu_ref, dw_ref,
    go, gate, up, w, pad, first, stage, mine, other, act, gfac,
    hidden_t, h_in, l_buf, sel_g, g_send, g_buf, d_send,
    load_sem, first_send, first_recv, zs, zr, ys, yr, hs, hr, ps, pr,
):
    rows, d = go.shape
    tokens, ff = gate.shape
    half, quarter = d // 2, d // 4
    fb = dw_ref.shape[1]
    f2 = 2 * fb
    ksize = 16 * nz
    width = quarter // SPLITS

    section = lax.axis_index("pipe")
    me = lax.axis_index("tensor")
    dp = lax.axis_index("dp")
    y, c = dp // 2, dp % 2

    def loads():
        return [
            pltpu.make_async_copy(go_hbm.at[0, 0], go, load_sem.at[0]),
            pltpu.make_async_copy(gate_hbm.at[0, 0], gate, load_sem.at[1]),
            pltpu.make_async_copy(up_hbm.at[0, 0], up, load_sem.at[2]),
            pltpu.make_async_copy(w_hbm.at[0], w, load_sem.at[3]),
        ]

    load_go, load_gate, load_up, load_w = loads()
    for one in (load_go, load_gate, load_up, load_w):
        one.start()

    right = lax.rem(me + 1, nz)
    left = lax.rem(me + nz - 1, nz)
    barrier = pltpu.get_barrier_semaphore()
    for k in range(1, 8):
        pl.semaphore_signal(barrier, inc=1, device_id={"dp": lax.rem(dp + k, 8)}, device_id_type=MESH)
    for z in (left, right):
        pl.semaphore_signal(barrier, inc=1, device_id={"tensor": z}, device_id_type=MESH)

    def place(core):
        even = 1 - lax.rem(y + 4 - core, 2)
        mate = lax.rem(y + 4 + 2 * even - 1, 4)
        outer = lax.rem(y + 4 - 2 * even + 1, 4)
        return 1 - even, mate, outer

    m_own, mate_own, outer_own = place(c)
    m_par, mate_par, _ = place(1 - c)
    q_own = 2 * m_own + c
    base_own = lax.rem(y + 4 - m_own, 4)
    partner = 2 * y + 1 - c

    load_go.wait()
    pad[...] = jnp.zeros_like(pad)
    for h in range(2):
        for u in range(2):
            at = h * half + u * quarter
            pad[h, 8 * u:8 * u + rows, :] = go[:, at:at + quarter].astype(F32)
    first[...] = pad[...].astype(BF16)

    pl.semaphore_wait(barrier, 9)

    def first_copy(target_dp, h, q, k):
        return pltpu.make_async_remote_copy(
            src_ref=first.at[h], dst_ref=stage.at[q], send_sem=first_send.at[k], recv_sem=first_recv.at[q],
            device_id={"dp": target_dp}, device_id_type=MESH,
        )

    firsts = [
        first_copy(2 * mate_own + c, c, q_own, 0),
        first_copy(2 * mate_par + 1 - c, 1 - c, 2 * m_par + c, 1),
        first_copy(partner, 1 - c, 2 * m_par + c, 2),
    ]
    for one in firsts:
        one.start()
    stage[q_own] = first[c]

    load_gate.wait()
    load_up.wait()
    g32 = gate[...].astype(F32)
    u32 = up[...].astype(F32)
    logistic = 1.0 / (1.0 + jnp.exp(-g32))
    activated = g32 * logistic
    act[...] = activated
    gfac[...] = u32 * logistic * (1.0 + g32 * (1.0 - logistic))
    hidden_t[...] = jnp.transpose((activated * u32).astype(BF16).astype(F32)).astype(BF16)

    def h_copy(k, slot):
        to = lax.rem(y + k, 4)
        return pltpu.make_async_remote_copy(
            src_ref=hidden_t.at[pl.ds(pl.multiple_of(to * f2, 16), f2), :], dst_ref=h_in.at[c, slot],
            send_sem=hs.at[k], recv_sem=hr.at[slot],
            device_id={"dp": 2 * to + c}, device_id_type=MESH,
        )

    for k in (1, 2, 3):
        h_copy(k, y).start()
    h_in[c, y] = hidden_t[pl.ds(pl.multiple_of(y * f2, 16), f2), :]

    for k in (1, 2, 3):
        first_copy(partner, 0, lax.rem(q_own + k, 4), 0).wait_recv()

    r = lax.broadcasted_iota(jnp.int32, (48, 64), 0)
    k = lax.broadcasted_iota(jnp.int32, (48, 64), 1)
    low = r % 16
    rho = jnp.where(r < 32, low, 16 + low % 8)
    u_of = jnp.where(r < 32, r // 16, low // 8)
    source = (rho // rows) * 16 + 8 * u_of + rho % rows
    pick = (source == k).astype(F32).astype(BF16)
    built = mm(pick, stage[...].reshape(64, quarter)).astype(BF16)
    for j in range(3):
        mine[j, 0:16, :] = built[16 * j:16 * j + 16, :]

    def z_copy(direction, slot, later, j, s, step):
        return pltpu.make_async_remote_copy(
            src_ref=mine.at[j, pl.ds(pl.multiple_of(16 * slot, 16), 16), pl.ds(s * width, width)],
            dst_ref=mine.at[j, pl.ds(pl.multiple_of(16 * later, 16), 16), pl.ds(s * width, width)],
            send_sem=zs.at[direction, lax.rem(step, 2), j, s], recv_sem=zr.at[direction, step, j, s],
            device_id={"tensor": right if direction == 0 else left}, device_id_type=MESH,
        )

    def y_copy(direction, slot, step):
        at = pl.ds(pl.multiple_of(16 * slot, 16), 16)
        return pltpu.make_async_remote_copy(
            src_ref=mine.at[:, at, :], dst_ref=other.at[:, at, :],
            send_sem=ys.at[direction, lax.rem(step, 2)], recv_sem=yr.at[slot],
            device_id={"dp": 2 * outer_own + c}, device_id_type=MESH,
        )

    blocks = [(j, s) for j in range(3) for s in range(SPLITS)]
    for j, s in blocks:
        z_copy(0, 0, 1, j, s, 0).start()
        z_copy(1, 0, nz - 1, j, s, 0).start()
    y_copy(0, 0, 0).start()

    top = nz // 2

    def step(d, carry):
        for j, s in blocks:
            z_copy(0, d - 1, d, j, s, d - 1).wait_recv()
            z_copy(0, d - 1, d, j, s, d - 1).wait_send()
            z_copy(0, d, d + 1, j, s, d).start()
            z_copy(1, nz - d, nz - d, j, s, d - 1).wait_recv()
            z_copy(1, nz - d, nz - d, j, s, d - 1).wait_send()

            @pl.when(d < top - 1)
            def _():
                z_copy(1, nz - d, nz - d - 1, j, s, d).start()

        @pl.when(d >= 2)
        def _():
            y_copy(0, d, d).wait_send()

        @pl.when(d >= 3)
        def _():
            y_copy(1, d, d).wait_send()

        y_copy(0, d, d).start()
        y_copy(1, nz - d, d).start()
        return carry

    def run(start, stop):
        lax.fori_loop(start, stop, step, 0)

    run(1, min(3, top))

    for k in (1, 2, 3):
        h_copy(1, lax.rem(y + k, 4)).wait_recv()
    h_pass = pltpu.make_async_remote_copy(
        src_ref=h_in.at[c], dst_ref=h_in.at[c], send_sem=ps.at[0], recv_sem=pr.at[0],
        device_id={"dp": partner}, device_id_type=MESH,
    )
    h_pass.start()
    run(3, min(6, top))

    t = lax.broadcasted_iota(jnp.int32, (tokens, ksize), 0)
    col = lax.broadcasted_iota(jnp.int32, (tokens, ksize), 1)
    z_rows = lax.rem(me + nz - col // 16, nz) * rows
    low = col % 16

    def select(q, kind):
        if kind == 0:
            rho, valid = low, low >= 0
        else:
            rho, valid = 16 + low % 8, (low // 8) == (kind - 1)
        i = rho - rows * q
        hit = valid & (i >= 0) & (i < rows) & (t == z_rows + i)
        return jnp.where(hit, 1.0, 0.0).astype(BF16)

    for kind in range(3):
        for cc in range(2):
            sel_g[kind, cc * tokens:(cc + 1) * tokens, :] = select(2 * m_own + cc, kind)
    run(6, min(8, top))
    h_pass.wait_recv()
    for group in range(2):
        base = lax.rem(base_own + 2 * group, 4)
        for kind in range(3):
            total = None
            for q in ((0, 1, 2) if kind == 0 else (2, 3)):
                h_q = h_in[q % 2, lax.rem(base + q // 2, 4)]
                term = mm(h_q, select(q, kind))
                total = term if total is None else total + term
            l_buf[group, kind] = total.astype(BF16)
    run(8, top)

    for j, s in blocks:
        z_copy(0, top - 1, top, j, s, top - 1).wait_recv()
        z_copy(0, top - 1, top, j, s, top - 1).wait_send()
    y_copy(0, top, top).wait_send()
    y_copy(0, top, top).start()

    tile = 256 if quarter % 256 == 0 else 128
    tiles = quarter // tile
    here = pl.multiple_of(c * half, half)

    for u in range(2):
        @pl.loop(0, tiles)
        def _(n):
            at = pl.ds(pl.multiple_of(n * tile, tile), tile)
            got = mm(sel_g[0], mine[u, :, at]) + mm(sel_g[1 + u], mine[2, :, at])
            both = got.astype(BF16)
            top_rows, bottom_rows = both[:tokens], both[tokens:]
            own_rows = jnp.where(c == 0, top_rows.astype(F32), bottom_rows.astype(F32)).astype(BF16)
            par_rows = jnp.where(c == 0, bottom_rows.astype(F32), top_rows.astype(F32)).astype(BF16)
            g_buf[:, pl.ds(pl.multiple_of(here + u * quarter + n * tile, tile), tile)] = own_rows
            g_send[:, pl.ds(pl.multiple_of(u * quarter + n * tile, tile), tile)] = par_rows

    g_pass = pltpu.make_async_remote_copy(
        src_ref=g_send, dst_ref=g_buf.at[:, pl.ds(here, half)], send_sem=ps.at[1], recv_sem=pr.at[1],
        device_id={"dp": partner}, device_id_type=MESH,
    )
    g_pass.start()

    before = jnp.int32(0)
    for k in range(npipe):
        before = before + jnp.where(section >= k, layers_ref[k], 0)
    scale = jnp.sqrt(10.0 / jnp.full((1, 128), before, jnp.int32).astype(F32))[:, :1]
    norm_scale = scale / jnp.sqrt(jnp.full((1, 1), tokens * 8, F32))

    for slot in range(nz):
        y_copy(0, slot, 0).wait_recv()

    for u in range(2):
        @pl.loop(0, tiles)
        def _(n):
            at = pl.ds(pl.multiple_of(n * tile, tile), tile)
            total = mm(l_buf[0, 0], mine[u, :, at]) + mm(l_buf[0, 1 + u], mine[2, :, at])
            total = total + mm(l_buf[1, 0], other[u, :, at]) + mm(l_buf[1, 1 + u], other[2, :, at])
            total = total * norm_scale
            low_rows, high_rows = total[:fb], total[fb:]
            dw_ref[0, :, pl.ds(pl.multiple_of(here + u * quarter + n * tile, tile), tile)] = jnp.where(
                c == 0, low_rows, high_rows).astype(BF16)
            d_send[:, pl.ds(pl.multiple_of(u * quarter + n * tile, tile), tile)] = jnp.where(
                c == 0, high_rows, low_rows).astype(BF16)

    d_pass = pltpu.make_async_remote_copy(
        src_ref=d_send, dst_ref=dw_ref.at[0, :, pl.ds(here, half)], send_sem=ps.at[2], recv_sem=pr.at[2],
        device_id={"dp": partner}, device_id_type=MESH,
    )
    d_pass.start()

    load_w.wait()
    g_pass.wait_recv()
    at = 0
    while at < ff:
        n = min(256, ff - at)
        gh = scale * lax.dot_general(
            g_buf[...], w[at:at + n, :], (((1,), (1,)), ((), ())), preferred_element_type=F32)
        gg_ref[0, 0, :, at:at + n] = (gh * gfac[:, at:at + n]).astype(BF16)
        gu_ref[0, 0, :, at:at + n] = (gh * act[:, at:at + n]).astype(BF16)
        at += n

    y_copy(0, top, top).wait_send()
    y_copy(0, top, top - 1).wait_send()
    y_copy(1, top, top - 1).wait_send()
    if top > 2:
        y_copy(1, top, top - 2).wait_send()
    for one in firsts:
        one.wait_send()
    for k in (1, 2, 3):
        h_copy(k, y).wait_send()
    h_pass.wait_send()
    g_pass.wait_send()
    d_pass.wait()


def per_device(section_layers, grad_out, gate_act, up_act, down_weight, *, sizes):
    npipe, nz = sizes
    rows, d = grad_out.shape[2:]
    tokens, ff = gate_act.shape[2:]
    fb = ff // 8
    ksize = 16 * nz
    any_spec = pl.BlockSpec(memory_space=pl.ANY)
    vmem_spec = pl.BlockSpec(memory_space=pltpu.VMEM)
    return pl.pallas_call(
        functools.partial(kernel, nz, npipe),
        out_shape=(
            jax.ShapeDtypeStruct(gate_act.shape, BF16),
            jax.ShapeDtypeStruct(gate_act.shape, BF16),
            jax.ShapeDtypeStruct((1, fb, d), BF16),
        ),
        in_specs=[pl.BlockSpec(memory_space=pltpu.SMEM)] + [any_spec] * 4,
        out_specs=(vmem_spec,) * 3,
        scratch_shapes=[
            pltpu.VMEM((rows, d), BF16),
            pltpu.VMEM((tokens, ff), BF16),
            pltpu.VMEM((tokens, ff), BF16),
            pltpu.VMEM((ff, d), BF16),
            pltpu.VMEM((2, 16, d // 4), F32),
            pltpu.VMEM((2, 16, d // 4), BF16),
            pltpu.VMEM((4, 16, d // 4), BF16),
            pltpu.VMEM((3, ksize, d // 4), BF16),
            pltpu.VMEM((3, ksize, d // 4), BF16),
            pltpu.VMEM((tokens, ff), F32),
            pltpu.VMEM((tokens, ff), F32),
            pltpu.VMEM((ff, tokens), BF16),
            pltpu.VMEM((2, 4, 2 * fb, tokens), BF16),
            pltpu.VMEM((2, 3, 2 * fb, ksize), BF16),
            pltpu.VMEM((3, 2 * tokens, ksize), BF16),
            pltpu.VMEM((tokens, d // 2), BF16),
            pltpu.VMEM((tokens, d), BF16),
            pltpu.VMEM((fb, d // 2), BF16),
            pltpu.SemaphoreType.DMA((4,)),
            pltpu.SemaphoreType.DMA((3,)),
            pltpu.SemaphoreType.DMA((4,)),
            pltpu.SemaphoreType.DMA((2, 2, 3, SPLITS)),
            pltpu.SemaphoreType.DMA((2, nz // 2, 3, SPLITS)),
            pltpu.SemaphoreType.DMA((2, 2)),
            pltpu.SemaphoreType.DMA((nz,)),
            pltpu.SemaphoreType.DMA((4,)),
            pltpu.SemaphoreType.DMA((4,)),
            pltpu.SemaphoreType.DMA((3,)),
            pltpu.SemaphoreType.DMA((3,)),
        ],
        compiler_params=pltpu.CompilerParams(
            collective_id=0, has_side_effects=True, vmem_limit_bytes=60 * 2**20
        ),
    )(section_layers, grad_out, gate_act, up_act, down_weight)


def solution(mesh):
    placed = (
        P(),
        P("pipe", "dp", "tensor", None),
        P("pipe", "dp", None, "tensor"),
        P("pipe", "dp", None, "tensor"),
        P("pipe", "tensor", None),
    )
    return jax.shard_map(
        functools.partial(per_device, sizes=(mesh.shape["pipe"], mesh.shape["tensor"])),
        mesh=mesh,
        in_specs=placed,
        out_specs=(
            P("pipe", "dp", None, "tensor"),
            P("pipe", "dp", None, "tensor"),
            P("pipe", ("tensor", "dp"), None),
        ),
        check_vma=False,
    )
```

time: 232 us -> 96.2 us (0.41)
  waiting for transfers between devices: 196 us -> 0 us
  Pallas kernels: 0 us -> 89.4 us
  matrix products: 15.6 us -> 0 us
  between operations: 15.4 us -> 0.64 us
    all_gather x1 -> x0, waiting for transfers between devices: 149 us -> none  [per_device(): all_rows = lax.all_gather(grad_out[0, 0], 'tensor', axis=0, tiled=True)]
    pallas_call x0 -> x1, Pallas kernels: none -> 89.4 us  [per_device(): pl.pallas_call(functools.partial(kernel, nz, npipe), out_shape=(jax.Shape...]
    reduce_scatter x1 -> x0, waiting for transfers between devices: 47 us -> none  [per_device(): lax.psum_scatter((norm_scale * lax.dot_general(hidden, all_rows, (((0,),...]
    dot_general x2 -> x0, matrix products: 15.6 us -> none  [the longest x1 7.96 us: per_device(): lax.dot_general(hidden, all_rows, (((0,), (0,)), ((), ())), preferred_ele...]
    unnamed x5 -> x3, local copies, waits for them, and re-layouts: 3.45 us -> 5.64 us
  transfers between devices with their start and end apart: 2 -> 0, of which waited for: 2 -> 0; matrix products, arithmetic and copies ran while one was open for 4% -> 0% of each run, Pallas kernels for 0% -> 0%
where the time goes in v1:
time: 96.2 us; the launch traced here: 95.7 us
  Pallas kernels  89.4 us (93%)
  local copies, waits for them, and re-layouts  5.64 us (6%)
    pallas_call x1, Pallas kernels, per_device(): pl.pallas_call(functools.partial(kernel, nz, npipe), out_shape=(jax.Shape...  89.4 us
    unnamed x3, local copies, waits for them, and re-layouts  5.64 us

profile of v1, /device:TPU:6, one launch (start us, length us, event | category | flops | bytes accessed | tf_op | source)
XLA Modules:
  0.0 95.7 jit_solution(515010311141112400)
XLA Ops:
  0.6 89.4 %shard_map.76 = (bf16[1,1,192,896]{3,2,1,0:T(8,128)(2,1)}, bf16[1,1,192,896]{3,2,1,0:T(8,128)(2,1)}, bf16[1,112,4096]{2,1,0:T(8,128)(2,1)}) custom-call(s32[4]{0:T(128)} %layers_ref.1, bf16[1,1,6,4096]{3,2,1,0:T(8,128)(2,1)} %go_hbm.1, bf16[1,1,192,896]{3,2,1,0:T(8,128)(2,1)} %gate_hbm.1, bf16[1,1,192,896]{3,2,1,0:T(8,128)(2,1)} %up_hbm.1, ...), custom_call_target="tpu_custom_call" | custom-call | tf_op jit(solution)/shard_map/pallas_call | solution.py:315
  90.1 1.7 %copy.11 = bf16[1,1,192,896]{3,2,1,0:T(8,128)(2,1)} copy(bf16[1,1,192,896]{3,2,1,0:T(8,128)(2,1)} %get-tuple-element.6) | data formatting | bytes 688128
  91.8 1.7 %copy.12 = bf16[1,1,192,896]{3,2,1,0:T(8,128)(2,1)} copy(bf16[1,1,192,896]{3,2,1,0:T(8,128)(2,1)} %get-tuple-element.7) | data formatting | bytes 688128
  93.5 2.2 %copy.13 = bf16[1,112,4096]{2,1,0:T(8,128)(2,1)} copy(bf16[1,112,4096]{2,1,0:T(8,128)(2,1)} %get-tuple-element.8) | data formatting | bytes 1835008

commit v2 on v1

v2 whole, which is shorter than its diff:
```python
import functools

import jax
import jax.numpy as jnp
from jax import lax
from jax.experimental import pallas as pl
from jax.experimental.pallas import tpu as pltpu
from jax.sharding import PartitionSpec as P

MESH = pl.DeviceIdType.MESH
F32 = jnp.float32
BF16 = jnp.bfloat16
SPLITS = 4


def mm(a, b):
    return jnp.dot(a, b, preferred_element_type=F32)


def kernel(
    nz, npipe,
    layers_ref, go_hbm, gate_hbm, up_hbm, w_hbm,
    gg_ref, gu_ref, dw_ref,
    go, gate, up, w, pad, first, stage, mine, other, act, gfac,
    hidden_t, h_in, l_buf, sel_g, g_send, g_recv, g_buf, d_send, d_recv, d_own,
    load_sem, first_send, first_recv, zs, zr, ys, yr, hs, hr, ps, pr,
):
    rows, d_model = go.shape
    tokens, ff = gate.shape
    half = d_model // 2
    fb = dw_ref.shape[1]
    f2 = 2 * fb
    top = nz // 2
    ksize = 16 * top
    part = rows * top
    width = half // SPLITS

    section = lax.axis_index("pipe")
    me = lax.axis_index("tensor")
    dp = lax.axis_index("dp")
    y, c = dp // 2, dp % 2

    load_go = pltpu.make_async_copy(go_hbm.at[0, 0], go, load_sem.at[0])
    load_gate = pltpu.make_async_copy(gate_hbm.at[0, 0], gate, load_sem.at[1])
    load_up = pltpu.make_async_copy(up_hbm.at[0, 0], up, load_sem.at[2])
    load_w = pltpu.make_async_copy(w_hbm.at[0], w, load_sem.at[3])
    load_go.start()

    right = lax.rem(me + 1, nz)
    left = lax.rem(me + nz - 1, nz)
    ahead = jnp.where(c == 0, right, left)
    barrier = pltpu.get_barrier_semaphore()
    for k in range(1, 8):
        pl.semaphore_signal(barrier, inc=1, device_id={"dp": lax.rem(dp + k, 8)}, device_id_type=MESH)
    for z in (left, right):
        pl.semaphore_signal(barrier, inc=1, device_id={"tensor": z}, device_id_type=MESH)
    load_gate.start()
    load_up.start()

    def place(core):
        even = 1 - lax.rem(y + 4 - core, 2)
        mate = lax.rem(y + 4 + 2 * even - 1, 4)
        outer = lax.rem(y + 4 - 2 * even + 1, 4)
        return 1 - even, mate, outer

    m_own, mate_own, outer_own = place(c)
    m_par, mate_par, _ = place(1 - c)
    q_own = 2 * m_own + c
    q_par = 2 * m_own + 1 - c
    base_own = lax.rem(y + 4 - m_own, 4)
    partner = 2 * y + 1 - c

    pad[...] = jnp.zeros_like(pad)
    load_go.wait()
    for u in range(2):
        pad[8 * u:8 * u + rows, :] = go[:, u * half:(u + 1) * half].astype(F32)
    first[...] = pad[...].astype(BF16)

    pl.semaphore_wait(barrier, 9)

    def first_copy(target_dp, q, k):
        return pltpu.make_async_remote_copy(
            src_ref=first, dst_ref=stage.at[q], send_sem=first_send.at[k], recv_sem=first_recv.at[q],
            device_id={"dp": target_dp}, device_id_type=MESH,
        )

    firsts = [
        first_copy(2 * mate_own + c, q_own, 0),
        first_copy(2 * mate_par + 1 - c, 2 * m_par + c, 1),
        first_copy(partner, 2 * m_par + c, 2),
    ]
    for one in firsts:
        one.start()
    stage[q_own] = first[...]

    load_gate.wait()
    load_up.wait()
    g32 = gate[...].astype(F32)
    u32 = up[...].astype(F32)
    logistic = 1.0 / (1.0 + jnp.exp(-g32))
    activated = g32 * logistic
    act[...] = activated
    gfac[...] = u32 * logistic * (1.0 + g32 * (1.0 - logistic))

    for k in (1, 2, 3):
        first_copy(partner, lax.rem(q_own + k, 4), 0).wait_recv()

    def pos(d):
        return lax.rem(d + top + c, top + 1)

    def at_slot(d):
        return pl.ds(pl.multiple_of(16 * pos(d), 16), 16)

    r = lax.broadcasted_iota(jnp.int32, (48, 64), 0)
    k = lax.broadcasted_iota(jnp.int32, (48, 64), 1)
    low = r % 16
    rho = jnp.where(r < 32, low, 16 + low % 8)
    u_of = jnp.where(r < 32, r // 16, low // 8)
    source = (rho // rows) * 16 + 8 * u_of + rho % rows
    pick = (source == k).astype(F32).astype(BF16)
    built = mm(pick, stage[...].reshape(64, half)).astype(BF16)
    for j in range(3):
        mine[j, at_slot(0), :] = built[16 * j:16 * j + 16, :]

    def z_copy(d, j, s):
        cols = pl.ds(s * width, width)
        return pltpu.make_async_remote_copy(
            src_ref=mine.at[j, at_slot(d), cols], dst_ref=mine.at[j, at_slot(d + 1), cols],
            send_sem=zs.at[lax.rem(d, 2), j, s], recv_sem=zr.at[d, j, s],
            device_id={"tensor": ahead}, device_id_type=MESH,
        )

    def y_copy(d):
        return pltpu.make_async_remote_copy(
            src_ref=mine.at[:, at_slot(d), :], dst_ref=other.at[:, at_slot(d), :],
            send_sem=ys.at[lax.rem(d, 2)], recv_sem=yr.at[pos(d)],
            device_id={"dp": 2 * outer_own + c}, device_id_type=MESH,
        )

    blocks = [(j, s) for j in range(3) for s in range(SPLITS)]
    for j, s in blocks:
        z_copy(0, j, s).start()

    @pl.when(c == 1)
    def _():
        y_copy(0).start()

    load_w.start()

    hidden_t[...] = jnp.transpose((act[...] * up[...].astype(F32)).astype(BF16).astype(F32)).astype(BF16)

    def h_copy(k, slot):
        to = lax.rem(y + k, 4)
        return pltpu.make_async_remote_copy(
            src_ref=hidden_t.at[pl.ds(pl.multiple_of(to * f2, 16), f2), :], dst_ref=h_in.at[c, slot],
            send_sem=hs.at[k], recv_sem=hr.at[slot],
            device_id={"dp": 2 * to + c}, device_id_type=MESH,
        )

    for k in (1, 2, 3):
        h_copy(k, y).start()
    h_in[c, y] = hidden_t[pl.ds(pl.multiple_of(y * f2, 16), f2), :]

    def step(d, carry):
        for j, s in blocks:
            @pl.when(d >= 2)
            def _():
                z_copy(d, j, s).wait_send()

            z_copy(d - 1, j, s).wait_recv()

            @pl.when(d < top - c)
            def _():
                z_copy(d, j, s).start()

        @pl.when(d >= 3 - c)
        def _():
            y_copy(d).wait_send()

        y_copy(d).start()
        return carry

    def run(start, stop):
        lax.fori_loop(start, stop, step, 0)

    run(1, min(3, top))

    for k in (1, 2, 3):
        h_copy(1, lax.rem(y + k, 4)).wait_recv()
    h_pass = pltpu.make_async_remote_copy(
        src_ref=h_in.at[c], dst_ref=h_in.at[c], send_sem=ps.at[0], recv_sem=pr.at[0],
        device_id={"dp": partner}, device_id_type=MESH,
    )
    h_pass.start()
    run(3, min(6, top))

    def z_of(p, core):
        return lax.rem(jnp.where(core == 0, me + nz - 1 - p, me + p), nz)

    def select(count, q, kind, natural):
        t = lax.broadcasted_iota(jnp.int32, (count, ksize), 0)
        col = lax.broadcasted_iota(jnp.int32, (count, ksize), 1)
        low = col % 16
        p = col // 16
        start = (z_of(p, c) if natural else p) * rows
        if kind == 0:
            rho, valid = low, low >= 0
        else:
            rho, valid = 16 + low % 8, (low // 8) == (kind - 1)
        i = rho - rows * q
        hit = valid & (i >= 0) & (i < rows) & (t == start + i)
        return jnp.where(hit, 1.0, 0.0).astype(BF16)

    for kind in range(3):
        sel_g[kind, :tokens, :] = select(tokens, q_own, kind, True)
        sel_g[kind, tokens:, :] = select(part, q_par, kind, False)
    run(6, min(8, top))
    h_pass.wait_recv()
    for group in range(2):
        base = lax.rem(base_own + 2 * group, 4)
        for kind in range(3):
            total = None
            for q in ((0, 1, 2) if kind == 0 else (2, 3)):
                h_q = h_in[q % 2, lax.rem(base + q // 2, 4)]
                term = mm(h_q, select(tokens, q, kind, True))
                total = term if total is None else total + term
            l_buf[group, kind] = total.astype(BF16)
    run(8, top)

    @pl.when(c == 0)
    def _():
        for j, s in blocks:
            z_copy(top - 1, j, s).wait_recv()
        if top > 2:
            y_copy(top).wait_send()
        y_copy(top).start()

    tile = 256 if half % 256 == 0 else 128
    tiles = half // tile

    def tile_at(u, n):
        return pl.ds(pl.multiple_of(u * half + n * tile, tile), tile)

    for u in range(2):
        @pl.loop(0, tiles)
        def _(n):
            at = tile_at(0, n)
            got = mm(sel_g[0], mine[u, 0:ksize, at]) + mm(sel_g[1 + u], mine[2, 0:ksize, at])
            both = got.astype(BF16)
            g_buf[:, tile_at(u, n)] = both[:tokens]
            g_send[:, tile_at(u, n)] = both[tokens:]

    g_pass = pltpu.make_async_remote_copy(
        src_ref=g_send, dst_ref=g_recv, send_sem=ps.at[1], recv_sem=pr.at[1],
        device_id={"dp": partner}, device_id_type=MESH,
    )
    g_pass.start()

    before = jnp.int32(0)
    for k in range(npipe):
        before = before + jnp.where(section >= k, layers_ref[k], 0)
    scale = jnp.sqrt(10.0 / jnp.full((1, 128), before, jnp.int32).astype(F32))[:, :1]
    norm_scale = scale / jnp.sqrt(jnp.full((1, 1), tokens * 8, F32))

    for p in range(top):
        pltpu.make_async_remote_copy(
            src_ref=mine.at[:, 0:16, :], dst_ref=other.at[:, 16 * p:16 * p + 16, :],
            send_sem=ys.at[0], recv_sem=yr.at[p],
            device_id={"dp": 2 * outer_own + c}, device_id_type=MESH,
        ).wait_recv()

    for u in range(2):
        @pl.loop(0, tiles)
        def _(n):
            at = tile_at(0, n)
            total = mm(l_buf[0, 0], mine[u, 0:ksize, at]) + mm(l_buf[0, 1 + u], mine[2, 0:ksize, at])
            total = total + mm(l_buf[1, 0], other[u, 0:ksize, at]) + mm(l_buf[1, 1 + u], other[2, 0:ksize, at])
            total = total * norm_scale
            low_rows, high_rows = total[:fb], total[fb:]
            d_own[:, tile_at(u, n)] = jnp.where(c == 0, low_rows, high_rows)
            d_send[:, tile_at(u, n)] = jnp.where(c == 0, high_rows, low_rows).astype(BF16)

    d_pass = pltpu.make_async_remote_copy(
        src_ref=d_send, dst_ref=d_recv, send_sem=ps.at[2], recv_sem=pr.at[2],
        device_id={"dp": partner}, device_id_type=MESH,
    )
    d_pass.start()

    t = lax.broadcasted_iota(jnp.int32, (tokens, part), 0)
    col = lax.broadcasted_iota(jnp.int32, (tokens, part), 1)
    spread = jnp.where(t == z_of(col // rows, 1 - c) * rows + col % rows, 1.0, 0.0).astype(BF16)
    g_pass.wait_recv()

    @pl.loop(0, 2 * tiles)
    def _(n):
        at = tile_at(0, n)
        g_buf[:, at] = (g_buf[:, at].astype(F32) + mm(spread, g_recv[:, at])).astype(BF16)

    load_w.wait()
    at = 0
    while at < ff:
        n = min(256, ff - at)
        gh = scale * lax.dot_general(
            g_buf[...], w[at:at + n, :], (((1,), (1,)), ((), ())), preferred_element_type=F32)
        gg_ref[0, 0, :, at:at + n] = (gh * gfac[:, at:at + n]).astype(BF16)
        gu_ref[0, 0, :, at:at + n] = (gh * act[:, at:at + n]).astype(BF16)
        at += n

    d_pass.wait()

    @pl.loop(0, 2 * tiles)
    def _(n):
        at = tile_at(0, n)
        dw_ref[0, :, at] = (d_own[:, at] + d_recv[:, at].astype(F32)).astype(BF16)

    y_copy(0).wait_send()
    y_copy(1).wait_send()
    for j, s in blocks:
        z_copy(top, j, s).wait_send()

        @pl.when(c == 0)
        def _():
            z_copy(top - 1, j, s).wait_send()
    for one in firsts:
        one.wait_send()
    for k in (1, 2, 3):
        h_copy(k, y).wait_send()
    h_pass.wait_send()
    g_pass.wait_send()


def put_out(gg_ref, gu_ref, dw_ref, gg_hbm, gu_hbm, dw_hbm, sem):
    copies = [
        pltpu.make_async_copy(gg_ref, gg_hbm, sem.at[0]),
        pltpu.make_async_copy(gu_ref, gu_hbm, sem.at[1]),
        pltpu.make_async_copy(dw_ref, dw_hbm, sem.at[2]),
    ]
    for one in copies:
        one.start()
    for one in copies:
        one.wait()


def per_device(section_layers, grad_out, gate_act, up_act, down_weight, *, sizes):
    npipe, nz = sizes
    rows, d = grad_out.shape[2:]
    tokens, ff = gate_act.shape[2:]
    fb = ff // 8
    top = nz // 2
    ksize = 16 * top
    part = rows * top
    any_spec = pl.BlockSpec(memory_space=pltpu.HBM)
    vmem_spec = pl.BlockSpec(memory_space=pltpu.VMEM)
    outs = (
        jax.ShapeDtypeStruct(gate_act.shape, BF16),
        jax.ShapeDtypeStruct(gate_act.shape, BF16),
        jax.ShapeDtypeStruct((1, fb, d), BF16),
    )
    section_layers, grad_out, gate_act, up_act, down_weight = (
        pltpu.with_memory_space_constraint(x, pltpu.HBM) for x in (section_layers, grad_out, gate_act, up_act, down_weight))
    got = pl.pallas_call(
        functools.partial(kernel, nz, npipe),
        out_shape=outs,
        in_specs=[pl.BlockSpec(memory_space=pltpu.SMEM)] + [any_spec] * 4,
        out_specs=(vmem_spec,) * 3,
        scratch_shapes=[
            pltpu.VMEM((rows, d), BF16),
            pltpu.VMEM((tokens, ff), BF16),
            pltpu.VMEM((tokens, ff), BF16),
            pltpu.VMEM((ff, d), BF16),
            pltpu.VMEM((16, d // 2), F32),
            pltpu.VMEM((16, d // 2), BF16),
            pltpu.VMEM((4, 16, d // 2), BF16),
            pltpu.VMEM((3, ksize + 16, d // 2), BF16),
            pltpu.VMEM((3, ksize + 16, d // 2), BF16),
            pltpu.VMEM((tokens, ff), F32),
            pltpu.VMEM((tokens, ff), F32),
            pltpu.VMEM((ff, tokens), BF16),
            pltpu.VMEM((2, 4, 2 * fb, tokens), BF16),
            pltpu.VMEM((2, 3, 2 * fb, ksize), BF16),
            pltpu.VMEM((3, tokens + part, ksize), BF16),
            pltpu.VMEM((part, d), BF16),
            pltpu.VMEM((part, d), BF16),
            pltpu.VMEM((tokens, d), BF16),
            pltpu.VMEM((fb, d), BF16),
            pltpu.VMEM((fb, d), BF16),
            pltpu.VMEM((fb, d), F32),
            pltpu.SemaphoreType.DMA((4,)),
            pltpu.SemaphoreType.DMA((3,)),
            pltpu.SemaphoreType.DMA((4,)),
            pltpu.SemaphoreType.DMA((2, 3, SPLITS)),
            pltpu.SemaphoreType.DMA((top, 3, SPLITS)),
            pltpu.SemaphoreType.DMA((2,)),
            pltpu.SemaphoreType.DMA((top,)),
            pltpu.SemaphoreType.DMA((4,)),
            pltpu.SemaphoreType.DMA((4,)),
            pltpu.SemaphoreType.DMA((3,)),
            pltpu.SemaphoreType.DMA((3,)),
        ],
        compiler_params=pltpu.CompilerParams(
            collective_id=0, has_side_effects=True, vmem_limit_bytes=44 * 2**20
        ),
    )(section_layers, grad_out, gate_act, up_act, down_weight)
    return pl.pallas_call(
        put_out,
        out_shape=outs,
        in_specs=[vmem_spec] * 3,
        out_specs=(any_spec,) * 3,
        scratch_shapes=[pltpu.SemaphoreType.DMA((3,))],
        compiler_params=pltpu.CompilerParams(vmem_limit_bytes=8 * 2**20),
    )(*got)


def solution(mesh):
    placed = (
        P(),
        P("pipe", "dp", "tensor", None),
        P("pipe", "dp", None, "tensor"),
        P("pipe", "dp", None, "tensor"),
        P("pipe", "tensor", None),
    )
    return jax.shard_map(
        functools.partial(per_device, sizes=(mesh.shape["pipe"], mesh.shape["tensor"])),
        mesh=mesh,
        in_specs=placed,
        out_specs=(
            P("pipe", "dp", None, "tensor"),
            P("pipe", "dp", None, "tensor"),
            P("pipe", ("tensor", "dp"), None),
        ),
        check_vma=False,
    )
```

time: 96.2 us -> 92.5 us (0.962)
  local copies, waits for them, and re-layouts: 5.64 us -> 0 us
  Pallas kernels: 89.4 us -> 91.7 us
    unnamed x3 -> x0, local copies, waits for them, and re-layouts: 5.64 us -> none
    pallas_call x1 -> x2, Pallas kernels: 89.4 us -> 91.7 us  [the longest x1 90.5 us: per_device(): pl.pallas_call(functools.partial(kernel, nz, npipe), out_shape=outs, in_s...]
where the time goes in v2:
time: 92.5 us; the launch traced here: 92.3 us
  Pallas kernels  91.7 us (99%)
    pallas_call x1, Pallas kernels, per_device(): pl.pallas_call(functools.partial(kernel, nz, npipe), out_shape=outs, in_s...  90.5 us

profile of v2, /device:TPU:6, one launch (start us, length us, event | category | flops | bytes accessed | tf_op | source)
XLA Modules:
  0.0 92.3 jit_solution(3108662721185618708)
XLA Ops:
  0.6 90.5 %shard_map.76 = (bf16[1,1,192,896]{3,2,1,0:T(8,128)(2,1)S(1)}, bf16[1,1,192,896]{3,2,1,0:T(8,128)(2,1)S(1)}, bf16[1,112,4096]{2,1,0:T(8,128)(2,1)S(1)}) custom-call(s32[4]{0:T(128)} %layers_ref.1, bf16[1,1,6,4096]{3,2,1,0:T(8,128)(2,1)} %go_hbm.1, bf16[1,1,192,896]{3,2,1,0:T(8,128)(2,1)} %gate_hbm.1, bf16[1,1,192,896]{3,2,1,0:T(8,128)(2,1)} %up_hbm.1, ...), custom_call_target="tpu_custom_call" | custom-call | tf_op jit(solution)/shard_map/pallas_call | solution.py:361
  91.2 1.2 %shard_map.77 = (bf16[1,1,192,896]{3,2,1,0:T(8,128)(2,1)}, bf16[1,1,192,896]{3,2,1,0:T(8,128)(2,1)}, bf16[1,112,4096]{2,1,0:T(8,128)(2,1)}) custom-call(bf16[1,1,192,896]{3,2,1,0:T(8,128)(2,1)S(1)} %get-tuple-element.6.gg_ref, bf16[1,1,192,896]{3,2,1,0:T(8,128)(2,1)S(1)} %get-tuple-element.7.gu_ref, bf16[1,112,4096]{2,1,0:T(8,128)(2,1)S(1)} %get-tuple-element.8.dw_ref), custom_call_target="tpu_custom_call" | custom-call | tf_op jit(solution)/shard_map/pallas_call | solution.py:404

commit v3 on v2

--- a/solution.py
+++ b/solution.py
@@ -161,16 +161,14 @@
         h_copy(k, y).start()
     h_in[c, y] = hidden_t[pl.ds(pl.multiple_of(y * f2, 16), f2), :]
 
-    def step(d, carry):
+    def step(d, carry, last=False):
         for j, s in blocks:
-            @pl.when(d >= 2)
-            def _():
-                z_copy(d, j, s).wait_send()
-
             z_copy(d - 1, j, s).wait_recv()
-
-            @pl.when(d < top - c)
-            def _():
+            if last:
+                @pl.when(c == 0)
+                def _():
+                    z_copy(d, j, s).start()
+            else:
                 z_copy(d, j, s).start()
 
         @pl.when(d >= 3 - c)
@@ -178,12 +176,14 @@
             y_copy(d).wait_send()
 
         y_copy(d).start()
+        for j, s in blocks:
+            z_copy(d - 1, j, s).wait_send()
         return carry
 
     def run(start, stop):
         lax.fori_loop(start, stop, step, 0)
 
-    run(1, min(3, top))
+    run(1, min(3, top - 1))
 
     for k in (1, 2, 3):
         h_copy(1, lax.rem(y + k, 4)).wait_recv()
@@ -192,7 +192,7 @@
         device_id={"dp": partner}, device_id_type=MESH,
     )
     h_pass.start()
-    run(3, min(6, top))
+    run(3, min(6, top - 1))
 
     def z_of(p, core):
         return lax.rem(jnp.where(core == 0, me + nz - 1 - p, me + p), nz)
@@ -214,7 +214,7 @@
     for kind in range(3):
         sel_g[kind, :tokens, :] = select(tokens, q_own, kind, True)
         sel_g[kind, tokens:, :] = select(part, q_par, kind, False)
-    run(6, min(8, top))
+    run(6, min(8, top - 1))
     h_pass.wait_recv()
     for group in range(2):
         base = lax.rem(base_own + 2 * group, 4)
@@ -225,7 +225,8 @@
                 term = mm(h_q, select(tokens, q, kind, True))
                 total = term if total is None else total + term
             l_buf[group, kind] = total.astype(BF16)
-    run(8, top)
+    run(8, top - 1)
+    step(top - 1, 0, last=True)
 
     @pl.when(c == 0)
     def _():
@@ -315,12 +316,12 @@
 
     y_copy(0).wait_send()
     y_copy(1).wait_send()
-    for j, s in blocks:
-        z_copy(top, j, s).wait_send()
-
-        @pl.when(c == 0)
-        def _():
+
+    @pl.when(c == 0)
+    def _():
+        for j, s in blocks:
             z_copy(top - 1, j, s).wait_send()
+
     for one in firsts:
         one.wait_send()
     for k in (1, 2, 3):

time: 92.5 us -> 92.5 us (level)
  no operation moved by 1% of the time
where the time goes in v3:
time: 92.5 us; the launch traced here: 92.3 us
  Pallas kernels  91.7 us (99%)
    pallas_call x1, Pallas kernels, per_device(): pl.pallas_call(functools.partial(kernel, nz, npipe), out_shape=outs, in_s...  90.5 us

profile of v3, /device:TPU:6, one launch (start us, length us, event | category | flops | bytes accessed | tf_op | source)
XLA Modules:
  0.0 92.3 jit_solution(17001130412861490806)
XLA Ops:
  0.6 90.5 %shard_map.76 = (bf16[1,1,192,896]{3,2,1,0:T(8,128)(2,1)S(1)}, bf16[1,1,192,896]{3,2,1,0:T(8,128)(2,1)S(1)}, bf16[1,112,4096]{2,1,0:T(8,128)(2,1)S(1)}) custom-call(s32[4]{0:T(128)} %layers_ref.1, bf16[1,1,6,4096]{3,2,1,0:T(8,128)(2,1)} %go_hbm.1, bf16[1,1,192,896]{3,2,1,0:T(8,128)(2,1)} %gate_hbm.1, bf16[1,1,192,896]{3,2,1,0:T(8,128)(2,1)} %up_hbm.1, ...), custom_call_target="tpu_custom_call" | custom-call | tf_op jit(solution)/shard_map/pallas_call | solution.py:362
  91.1 1.2 %shard_map.77 = (bf16[1,1,192,896]{3,2,1,0:T(8,128)(2,1)}, bf16[1,1,192,896]{3,2,1,0:T(8,128)(2,1)}, bf16[1,112,4096]{2,1,0:T(8,128)(2,1)}) custom-call(bf16[1,1,192,896]{3,2,1,0:T(8,128)(2,1)S(1)} %get-tuple-element.6.gg_ref, bf16[1,1,192,896]{3,2,1,0:T(8,128)(2,1)S(1)} %get-tuple-element.7.gu_ref, bf16[1,112,4096]{2,1,0:T(8,128)(2,1)S(1)} %get-tuple-element.8.dw_ref), custom_call_target="tpu_custom_call" | custom-call | tf_op jit(solution)/shard_map/pallas_call | solution.py:405
